TPU v7x, 32 devices: a whole 2x2x4 slice. The times are simulated.
32 devices in a mesh: groups: 2 (over x), slab: 16 (over z, y, core).
Axes of the slice: x: 2, y: 2, z: 4, core: 2. Of those that a mesh axis runs over, the one named last changes fastest.
Arguments:
- wavefields: float32 [2, 4, 4, 2048, 512], P(None, None, 'groups', 'slab'), parts along dimension 2, may hold values from -6 to 6
- courant: float32 [2048, 512], P('slab'), may hold values from 0.04 to 0.16
- epsilon: float32 [2048, 512], P('slab'), may hold values from 0.1 to 0.3
- anisotropy_delta: float32 [2048, 512], P('slab'), may hold values from 0 to 0.1
- tilt_angle: float32 [2048, 512], P('slab'), may hold values from -3.140625 to 3.140625
- loc_patch: int32 [256], replicated, may hold values from 0 to 63, as said below
- slab_counts: int32 [16], replicated, may hold values from 3 to 4
- angle_table: int32 [64], replicated, may hold values from -48 to 47
Outputs:
- gathers: float32 [512, 4096], P(('groups', 'slab')), parts along dimension 0
There are 2 independent parts, one for each index of `groups`. A program takes and returns all parts, laid end to end along the dimension named above; an argument that names none is the same for every part. Nothing has to cross between parts.
Inputs may be any that keep to these rules, and one draw needn't show every extreme that they name: `loc_patch`: location g names a patch id slab * 4 + column block; locations g of one owner are the 16 rows of an aligned block. Within one block no slab is named by more than 2 locations, and some slab is named by exactly 2 in every block.
All inputs are finite; a program needn't handle non-finite values.
Results may differ from a plain program's by a relative error of at most 0.0055.
Values may be sent and summed in bfloat16 or wider, within the bound.
A program may use at most 128 MiB of HBM per device.

v0:
```python
import math

import jax
import jax.numpy as jnp
from jax import lax
from jax.sharding import PartitionSpec as P

STEPS = 2
CAP = 2


SECOND_TERMS = (-205.0 / 72.0, 8.0 / 5.0, -1.0 / 5.0, 8.0 / 315.0, -1.0 / 560.0)
FIRST_TERMS = (4.0 / 5.0, -1.0 / 5.0, 4.0 / 105.0, -1.0 / 280.0)


def padded(array, sides, width):
    for axis, dim in sides:
        size, length = (lax.axis_size(axis), array.shape[dim])
        up = [(i, (i + 1) % size) for i in range(size - 1)]
        down = [(j, i) for i, j in up]
        last = lax.slice_in_dim(array, length - width, length, axis=dim)
        leading = lax.slice_in_dim(array, 0, width, axis=dim)
        before = lax.ppermute(last, axis, up)
        after = lax.ppermute(leading, axis, down)
        array = jnp.concatenate([before, array, after], axis=dim)
    return array


def pad_columns(field):
    widths = [(0, 0)] * (field.ndim - 1) + [(4, 4)]
    return jnp.pad(field, widths)


def derivatives(field):
    row_count = field.shape[-2] - 8
    column_count = field.shape[-1]
    middle = field[..., 4 : 4 + row_count, :]
    beside = pad_columns(middle)
    second_z = SECOND_TERMS[0] * middle
    second_x = SECOND_TERMS[0] * middle
    first_z = jnp.zeros_like(middle)
    for offset in range(1, 5):
        upper_rows = field[..., 4 + offset : 4 + offset + row_count, :]
        lower_rows = field[..., 4 - offset : 4 - offset + row_count, :]
        second_z = second_z + SECOND_TERMS[offset] * (upper_rows + lower_rows)
        first_z = first_z + FIRST_TERMS[offset - 1] * (upper_rows - lower_rows)
        second_x = second_x + SECOND_TERMS[offset] * (
            beside[..., 4 + offset : 4 + offset + column_count]
            + beside[..., 4 - offset : 4 - offset + column_count]
        )
    spread = pad_columns(first_z)
    mixed_term = jnp.zeros_like(middle)
    for offset in range(1, 5):
        mixed_term = mixed_term + FIRST_TERMS[offset - 1] * (
            spread[..., 4 + offset : 4 + offset + column_count]
            - spread[..., 4 - offset : 4 - offset + column_count]
        )
    return (second_x, second_z, mixed_term)


def advance(current, previous, courant, epsilon, anisotropy_delta, tilt_angle):
    second_x, second_z, mixed_term = derivatives(current)
    sine_tilt = jnp.sin(tilt_angle)
    cosine = jnp.cos(tilt_angle)
    along_axis = (
        sine_tilt * sine_tilt * second_x
        + cosine * cosine * second_z
        + 2.0 * sine_tilt * cosine * mixed_term
    )
    across = second_x + second_z - along_axis
    root_delta = jnp.sqrt(1.0 + 2.0 * anisotropy_delta)
    push_pressure = (1.0 + 2.0 * epsilon) * across[:, 0] + root_delta * along_axis[:, 1]
    push_other = root_delta * across[:, 0] + along_axis[:, 1]
    middle = current[..., 4:-4, :]
    return 2.0 * middle - previous + courant * jnp.stack([push_pressure, push_other], axis=1)


def depth_table(patch, bins):
    wavenumber = jnp.arange(bins, dtype=jnp.int32)[:, None]
    depth_index = jnp.arange(patch, dtype=jnp.int32)[None, :]
    phase = 2.0 * math.pi / patch * jnp.mod(wavenumber * depth_index, patch).astype(jnp.float32)
    scale = 1.0 / math.sqrt(patch)
    return jnp.concatenate([jnp.cos(phase), -jnp.sin(phase)], axis=0) * scale


def slant_table(angle_table, patch, bins):
    wavenumber = jnp.arange(bins, dtype=jnp.int32)[:, None, None]
    lateral = jnp.arange(patch, dtype=jnp.int32)[None, None, :]
    slopes = angle_table[None, :, None]
    modulus = 16 * patch
    phase = (
        2.0
        * math.pi
        / modulus
        * jnp.mod(wavenumber * slopes * lateral, modulus).astype(jnp.float32)
    )
    scale = 1.0 / math.sqrt(patch)
    real_part = jnp.cos(phase) * scale
    imag_part = -jnp.sin(phase) * scale
    upper_half = jnp.stack([real_part, -imag_part], axis=2)
    lower_half = jnp.stack([imag_part, real_part], axis=2)
    return jnp.concatenate([upper_half, lower_half], axis=1).astype(jnp.bfloat16)


def correlate(stacked, angles):
    shaped = stacked.reshape(stacked.shape[:-1] + (2, angles))
    product = shaped[..., 0, :, :, :, :] * shaped[..., 1, :, :, :, :]
    summed = jnp.sum(product, axis=(-4, -2))
    return summed.reshape(summed.shape[:-2] + (summed.shape[-2] * angles,))


def per_device(
    wavefields, courant, epsilon, anisotropy_delta, tilt_angle, loc_patch, slab_counts, angle_table
):
    slab_total = lax.axis_size("slab")
    slab_index = lax.axis_index("slab")
    slab_rows = wavefields.shape[3]
    lateral_cells = wavefields.shape[4]
    shot_count = wavefields.shape[2]
    bins = slab_rows // 2
    angles = angle_table.shape[0]
    per_slab = lateral_cells // slab_rows
    current = wavefields[:, 0:2]
    previous = wavefields[:, 2:4]
    for iteration in range(STEPS):
        extended = padded(current, (("slab", 3),), 4)
        current, previous = (
            advance(extended, previous, courant, epsilon, anisotropy_delta, tilt_angle),
            current,
        )
    pressure = current[:, 0]
    table = depth_table(slab_rows, bins)
    spectra = jnp.einsum("qz,fszx->fsqx", table, pressure, precision=lax.Precision.HIGHEST).astype(
        jnp.bfloat16
    )
    spectra = spectra.reshape(2, shot_count, 2, bins, per_slab, slab_rows)
    slant = slant_table(angle_table, slab_rows, bins)
    blocks = loc_patch.reshape(slab_total, -1)
    block_size = blocks.shape[1]
    owner_slab = blocks // per_slab
    column = blocks % per_slab
    order_ids = jnp.arange(block_size, dtype=jnp.int32)
    earlier = (owner_slab[:, :, None] == owner_slab[:, None, :]) & (
        order_ids[None, None, :] < order_ids[None, :, None]
    )
    ranks = jnp.sum(earlier.astype(jnp.int32), axis=2)
    slab_ids = jnp.arange(slab_total, dtype=jnp.int32)
    counts_of = jnp.sum(jnp.where(owner_slab[..., None] == slab_ids, slab_counts, 0), axis=-1)
    alive = column < counts_of
    mine = ((owner_slab == slab_index) & alive).astype(jnp.float32)
    slot_ids = jnp.arange(CAP, dtype=jnp.int32)
    rank_hot = (ranks[..., None] == slot_ids).astype(jnp.float32)
    column_hot = (column[..., None] == jnp.arange(per_slab, dtype=jnp.int32)).astype(jnp.float32)
    chooser = jnp.einsum("dj,djc,djp->dcp", mine, rank_hot, column_hot)
    stacked = jnp.einsum("kirx,fsrkpx->pfski", slant, spectra, preferred_element_type=jnp.float32)
    own_images = correlate(stacked, angles)
    payload = jnp.einsum("dcp,po->dco", chooser, own_images, precision=lax.Precision.HIGHEST)
    images = lax.all_to_all(payload, "slab", split_axis=0, concat_axis=0, tiled=True)
    my_slabs = lax.dynamic_index_in_dim(owner_slab, slab_index, 0, keepdims=False)
    my_ranks = lax.dynamic_index_in_dim(ranks, slab_index, 0, keepdims=False)
    picker = (
        (my_slabs[:, None, None] == slab_ids[None, :, None])
        & (my_ranks[:, None, None] == slot_ids[None, None, :])
    ).astype(jnp.float32)
    return jnp.einsum("jnc,nco->jo", picker, images, precision=lax.Precision.HIGHEST)


def solution(mesh):
    return jax.shard_map(
        per_device,
        mesh=mesh,
        in_specs=(
            P(None, None, "groups", "slab", None),
            P("slab", None),
            P("slab", None),
            P("slab", None),
            P("slab", None),
            P(),
            P(),
            P(),
        ),
        out_specs=P(("groups", "slab"), None),
        check_vma=False,
    )
```

profile of v0, /device:TPU:0, one launch (start us, length us, event | category | flops | bytes accessed | tf_op | source)
XLA Modules:
  0.0 144.0 jit_solution(1743047643772985181)
XLA Ops:
  0.0 1.6 %fusion.63 = (f32[2,2,2,4,512]{4,3,2,1,0:T(4,128)}, f32[2,2,2,4,512]{4,3,2,1,0:T(4,128)}) fusion(f32[2,4,2,128,512]{4,3,2,1,0:T(8,128)} %param.8), kind=kLoop, calls=%fused_computation.144 | loop fusion | bytes 262144 | tf_op jit(solution)/shard_map/slice | solution.py:21
  1.6 1.3 collective-permute-start
  3.0 3.2 %collective-permute-start.1 = (f32[2,2,2,4,512]{4,3,2,1,0:T(4,128)}, f32[2,2,2,4,512]{4,3,2,1,0:T(4,128)S(1)}, u32[]{:S(2)}, u32[]{:S(2)}) collective-permute-start(f32[2,2,2,4,512]{4,3,2,1,0:T(4,128)} %get-tuple-element.19), channel_id=1, source_target_pairs={{0,1},{1,2},{2,3},{3,4},{4,5},{5,6},{6,7},{7,8},{8,9},{9,10},{10,1... | collective-permute-start | bytes 196616 | tf_op jit(solution)/shard_map/ppermute | solution.py:23
  6.1 4.8 %fusion.62 = (f32[2,2,2,128,512]{4,3,2,1,0:T(8,128)}, f32[2,2,2,128,512]{4,3,2,1,0:T(8,128)}) fusion(f32[2,4,2,128,512]{4,3,2,1,0:T(8,128)} %param.8), kind=kLoop, calls=%fused_computation.143 | loop fusion | bytes 8388608 | tf_op jit(solution)/shard_map/slice | solution.py:124
  11.0 1.0 fusion.65
  13.5 11.0 %negate_convert_fusion = (bf16[64,64,1,128]{3,1,2,0:T(8,128)(2,1)}, bf16[64,64,1,128]{3,1,2,0:T(8,128)(2,1)}, bf16[64,64,1,128]{3,1,2,0:T(8,128)(2,1)}) fusion(s32[64,64]{1,0:T(8,128)S(1)} %iota_multiply_fusion), kind=kLoop, calls=%fused_computation.51 | loop fusion | flops 11010048 | bytes 3162112 | tf_op jit(solution)/shard_map/convert.7
  26.2 1.9 %copy.96 = f32[2,2,2,128,512]{3,4,2,0,1:T(8,128)S(1)} copy(f32[2,2,2,128,512]{4,3,2,1,0:T(8,128)} %get-tuple-element.18) | data formatting | bytes 4194304
  28.6 1.3 copy.74
  29.8 1.8 %copy.80 = f32[128,512]{0,1:T(8,128)} copy(f32[128,512]{1,0:T(8,128)} %add_sqrt_fusion) | data formatting | bytes 524288 | tf_op jit(solution)/shard_map/sqrt | solution.py:71
  31.6 2.9 %copy.97 = f32[2,2,2,128,512]{3,4,2,0,1:T(8,128)} copy(f32[2,2,2,128,512]{4,3,2,1,0:T(8,128)} %get-tuple-element.17) | data formatting | bytes 4194304
  34.6 1.1 copy.73
  35.6 1.9 %copy.75 = f32[2,2,2,4,512]{3,4,2,0,1:T(8,128)} copy(f32[2,2,2,4,512]{4,3,2,1,0:T(4,128)S(1)} %collective-permute-done) | data formatting | bytes 131072 | tf_op jit(solution)/shard_map/ppermute | solution.py:24
  37.6 2.0 %copy.76 = f32[2,2,2,4,512]{3,4,2,0,1:T(8,128)} copy(f32[2,2,2,4,512]{4,3,2,1,0:T(4,128)S(1)} %collective-permute-done.1) | data formatting | bytes 131072 | tf_op jit(solution)/shard_map/ppermute | solution.py:23
  39.6 14.4 %multiply_add_fusion.5 = f32[2,2,2,128,512]{3,4,2,0,1:T(8,128)S(1)} fusion(f32[2,2,2,4,512]{3,4,2,0,1:T(8,128)} %copy.75, f32[2,2,2,128,512]{3,4,2,0,1:T(8,128)S(1)} %copy.96, f32[2,2,2,4,512]{3,4,2,0,1:T(8,128)} %copy.76), kind=kLoop, calls=%fused_computation.61 | loop fusion | flops 9961472 | bytes 4325376 | tf_op jit(solution)/shard_map/add | solution.py:46
  54.1 8.7 %multiply_add_fusion.4 = (f32[2,2,2,128,512]{3,4,2,0,1:T(8,128)S(1)}, f32[2,2,2,128,512]{3,4,2,0,1:T(8,128)S(1)}, f32[2,2,2,128,512]{3,4,2,0,1:T(8,128)S(1)}) fusion(f32[2,2,2,128,512]{3,4,2,0,1:T(8,128)S(1)} %multiply_add_fusion.5, f32[128,512]{0,1:T(8,128)S(1)} %copy.79, f32[128,512]{0,1:T(8,128)S(1)} %copy.78, f32[128,512]{0,1:T(8,128)S(1)} %copy.77, ...), kind=kLoop, calls=%fused_computation.60 | loop fusion | flops 25690112 | bytes 11403264 | tf_op jit(solution)/shard_map/add | solution.py:66
  62.8 1.4 multiply_add_fusion.11
  65.5 2.7 %fusion.64 = (f32[2,2,2,4,512]{3,4,2,0,1:T(8,128)}, f32[2,2,2,4,512]{3,4,2,0,1:T(8,128)}) fusion(f32[2,2,2,128,512]{3,4,2,0,1:T(8,128)S(1)} %fusion.16), kind=kLoop, calls=%fused_computation.145 | loop fusion | bytes 262144 | tf_op jit(solution)/shard_map/slice | solution.py:21
  68.2 2.2 %copy.81 = f32[2,2,2,4,512]{4,3,2,1,0:T(4,128)S(1)} copy(f32[2,2,2,4,512]{3,4,2,0,1:T(8,128)} %get-tuple-element.22) | data formatting | bytes 131072 | tf_op jit(solution)/shard_map/slice | solution.py:22
  70.4 1.3 collective-permute-start.2
  71.7 2.8 %copy.83 = f32[2,2,2,4,512]{4,3,2,1,0:T(4,128)} copy(f32[2,2,2,4,512]{3,4,2,0,1:T(8,128)} %get-tuple-element.21) | data formatting | bytes 131072 | tf_op jit(solution)/shard_map/slice | solution.py:21
  74.6 5.8 %collective-permute-start.3 = (f32[2,2,2,4,512]{4,3,2,1,0:T(4,128)}, f32[2,2,2,4,512]{4,3,2,1,0:T(4,128)}, u32[]{:S(2)}, u32[]{:S(2)}) collective-permute-start(f32[2,2,2,4,512]{4,3,2,1,0:T(4,128)} %copy.83), channel_id=1, source_target_pairs={{0,1},{1,2},{2,3},{3,4},{4,5},{5,6},{6,7},{7,8},{8,9},{9,10},{10,1... | collective-permute-start | bytes 196616 | tf_op jit(solution)/shard_map/ppermute | solution.py:23
  80.5 2.8 %copy.82 = f32[2,2,2,4,512]{3,4,2,0,1:T(8,128)} copy(f32[2,2,2,4,512]{4,3,2,1,0:T(4,128)} %collective-permute-done.2) | data formatting | bytes 131072 | tf_op jit(solution)/shard_map/ppermute | solution.py:24
  83.3 2.8 %copy.84 = f32[2,2,2,4,512]{3,4,2,0,1:T(8,128)} copy(f32[2,2,2,4,512]{4,3,2,1,0:T(4,128)} %collective-permute-done.3) | data formatting | bytes 131072 | tf_op jit(solution)/shard_map/ppermute | solution.py:23
  86.1 14.9 %multiply_add_fusion.1 = f32[2,2,2,128,512]{3,4,2,0,1:T(8,128)S(1)} fusion(f32[2,2,2,4,512]{3,4,2,0,1:T(8,128)} %copy.82, f32[2,2,2,128,512]{3,4,2,0,1:T(8,128)S(1)} %fusion.16, f32[2,2,2,4,512]{3,4,2,0,1:T(8,128)} %copy.84), kind=kLoop, calls=%fused_computation.57 | loop fusion | flops 9961472 | bytes 4325376 | tf_op jit(solution)/shard_map/add | solution.py:46
  101.0 8.7 %multiply_add_fusion = (f32[2,2,2,128,512]{3,4,2,0,1:T(8,128)S(1)}, f32[2,2,2,128,512]{3,4,2,0,1:T(8,128)S(1)}, f32[2,2,2,128,512]{3,4,2,0,1:T(8,128)S(1)}) fusion(f32[2,2,2,128,512]{3,4,2,0,1:T(8,128)S(1)} %multiply_add_fusion.1, f32[128,512]{0,1:T(8,128)S(1)} %copy.79, f32[128,512]{0,1:T(8,128)S(1)} %copy.78, f32[128,512]{0,1:T(8,128)S(1)} %copy.77, ...), kind=kLoop, calls=%fused_computation.56 | loop fusion | flops 25690112 | bytes 11403264 | tf_op jit(solution)/shard_map/add | solution.py:66
  109.7 1.4 multiply_add_fusion.9
  111.4 1.1 fusion.22
  113.8 3.0 %fusion.21 = f32[4,2,2,64,128]{4,0,2,1,3:T(4,128)S(1)} fusion(bf16[2,2,2,64,4,128]{5,4,2,1,0,3:T(4,128)(2,1)S(1)} %copy.86, bf16[64,64,1,128]{3,1,2,0:T(8,128)(2,1)} %get-tuple-element.30, bf16[64,64,1,128]{3,1,2,0:T(8,128)(2,1)} %get-tuple-element.29, bf16[64,64,1,128]{3,1,2,0:T(8,128)(2,1)S(1)} %copy-done.8), kind=kOutput, calls=%fused_computation.67 | convolution fusion | flops 83886080 | bytes 4194304 | tf_op jit(solution)/shard_map/kirx,fsrkpx->pfski/dot_general | solution.py:155
  119.0 1.2 copy.89
  120.2 8.1 %all-to-all-start = ((f32[16,2,4096]{2,1,0:T(2,128)}), f32[16,2,4096]{2,1,0:T(2,128)S(1)}, u32[]{:S(2)}, u32[]{:S(2)}) async-start(f32[16,2,4096]{2,1,0:T(2,128)} %copy.89), calls=%async_computation | async-start | bytes 1048576 | tf_op jit(solution)/shard_map/all_to_all | solution.py:158
  128.4 14.2 %all-to-all-done = f32[16,2,4096]{2,1,0:T(2,128)S(1)} async-done(((f32[16,2,4096]{2,1,0:T(2,128)}), f32[16,2,4096]{2,1,0:T(2,128)S(1)}, u32[]{:S(2)}, u32[]{:S(2)}) %all-to-all-start) | async-done | bytes 524320 | tf_op jit(solution)/shard_map/all_to_all | solution.py:158
  142.6 1.4 convolution_bitcast_fusion
  (61 shorter events, 8.7 us)
Async XLA Ops:
  1.6 34.0 %collective-permute-start = (f32[2,2,2,4,512]{4,3,2,1,0:T(4,128)}, f32[2,2,2,4,512]{4,3,2,1,0:T(4,128)S(1)}, u32[]{:S(2)}, u32[]{:S(2)}) collective-permute-start(f32[2,2,2,4,512]{4,3,2,1,0:T(4,128)} %get-tuple-element.20), channel_id=1, source_target_pairs={{1,0},{2,1},{3,2},{4,3},{5,4},{6,5},{7,6},{8,7},{9,8},{10,9},{11,1... | collective-permute-start | bytes 196616 | tf_op jit(solution)/shard_map/ppermute | solution.py:24
  2.9 8.1 %copy-start.9 = (f32[128,512]{1,0:T(8,128)S(1)}, f32[128,512]{1,0:T(8,128)}, u32[]{:S(2)}) copy-start(f32[128,512]{1,0:T(8,128)} %param.12) | copy-start | bytes 786436
  2.9 9.0 %copy-start.10 = (f32[128,512]{1,0:T(8,128)S(1)}, f32[128,512]{1,0:T(8,128)}, u32[]{:S(2)}) copy-start(f32[128,512]{1,0:T(8,128)} %param.10) | copy-start | bytes 786436
  3.0 9.8 %copy-start.11 = (f32[128,512]{1,0:T(8,128)S(1)}, f32[128,512]{1,0:T(8,128)}, u32[]{:S(2)}) copy-start(f32[128,512]{1,0:T(8,128)} %param.11) | copy-start | bytes 786436
  3.0 10.6 %copy-start.14 = (s32[64]{0:T(128)S(1)}, s32[64]{0:T(128)}, u32[]{:S(2)}) copy-start(s32[64]{0:T(128)} %param.15) | copy-start | bytes 772
  3.0 34.6 %collective-permute-start.1 = (f32[2,2,2,4,512]{4,3,2,1,0:T(4,128)}, f32[2,2,2,4,512]{4,3,2,1,0:T(4,128)S(1)}, u32[]{:S(2)}, u32[]{:S(2)}) collective-permute-start(f32[2,2,2,4,512]{4,3,2,1,0:T(4,128)} %get-tuple-element.19), channel_id=1, source_target_pairs={{0,1},{1,2},{2,3},{3,4},{4,5},{5,6},{6,7},{7,8},{8,9},{9,10},{10,1... | collective-permute-start | bytes 196616 | tf_op jit(solution)/shard_map/ppermute | solution.py:23
  12.0 12.6 %copy-start.13 = (s32[256]{0:T(256)S(1)}, s32[256]{0:T(256)}, u32[]{:S(2)}) copy-start(s32[256]{0:T(256)} %param.13) | copy-start | bytes 3076
  13.5 11.2 %copy-start.15 = (s32[16]{0:T(128)S(1)}, s32[16]{0:T(128)}, u32[]{:S(2)}) copy-start(s32[16]{0:T(128)} %param.14) | copy-start | bytes 196
  28.1 25.9 %copy-start = (f32[2,2,2,128,512]{3,4,2,0,1:T(8,128)}, f32[2,2,2,128,512]{3,4,2,0,1:T(8,128)S(1)}, u32[]{:S(2)}) copy-start(f32[2,2,2,128,512]{3,4,2,0,1:T(8,128)S(1)} %copy.96) | copy-start | bytes 6291460
  39.6 14.4 %copy-start.4 = (f32[2,2,2,4,512]{3,4,2,0,1:T(8,128)S(1)}, f32[2,2,2,4,512]{3,4,2,0,1:T(8,128)}, u32[]{:S(2)}) copy-start(f32[2,2,2,4,512]{3,4,2,0,1:T(8,128)} %copy.75) | copy-start | bytes 196612
  39.6 14.4 %copy-start.6 = (f32[2,2,2,4,512]{3,4,2,0,1:T(8,128)S(1)}, f32[2,2,2,4,512]{3,4,2,0,1:T(8,128)}, u32[]{:S(2)}) copy-start(f32[2,2,2,4,512]{3,4,2,0,1:T(8,128)} %copy.76) | copy-start | bytes 196612
  62.8 1.7 %copy-start.1 = (f32[2,2,2,128,512]{3,4,2,0,1:T(8,128)S(1)}, f32[2,2,2,128,512]{3,4,2,0,1:T(8,128)}, u32[]{:S(2)}) copy-start(f32[2,2,2,128,512]{3,4,2,0,1:T(8,128)} %copy-done) | copy-start | bytes 6291460
  62.8 2.3 %copy-start.7 = (f32[2,2,2,128,512]{3,4,2,0,1:T(8,128)S(1)}, f32[2,2,2,128,512]{3,4,2,0,1:T(8,128)}, u32[]{:S(2)}) copy-start(f32[2,2,2,128,512]{3,4,2,0,1:T(8,128)} %copy.97) | copy-start | bytes 6291460
  70.4 10.1 %collective-permute-start.2 = (f32[2,2,2,4,512]{4,3,2,1,0:T(4,128)S(1)}, f32[2,2,2,4,512]{4,3,2,1,0:T(4,128)}, u32[]{:S(2)}, u32[]{:S(2)}) collective-permute-start(f32[2,2,2,4,512]{4,3,2,1,0:T(4,128)S(1)} %copy.81), channel_id=1, source_target_pairs={{1,0},{2,1},{3,2},{4,3},{5,4},{6,5},{7,6},{8,7},{9,8},{10,9},{11,1... | collective-permute-start | bytes 196616 | tf_op jit(solution)/shard_map/ppermute | solution.py:24
  74.6 8.7 %collective-permute-start.3 = (f32[2,2,2,4,512]{4,3,2,1,0:T(4,128)}, f32[2,2,2,4,512]{4,3,2,1,0:T(4,128)}, u32[]{:S(2)}, u32[]{:S(2)}) collective-permute-start(f32[2,2,2,4,512]{4,3,2,1,0:T(4,128)} %copy.83), channel_id=1, source_target_pairs={{0,1},{1,2},{2,3},{3,4},{4,5},{5,6},{6,7},{7,8},{8,9},{9,10},{10,1... | collective-permute-start | bytes 196616 | tf_op jit(solution)/shard_map/ppermute | solution.py:23
  86.1 14.9 %copy-start.3 = (f32[2,2,2,4,512]{3,4,2,0,1:T(8,128)S(1)}, f32[2,2,2,4,512]{3,4,2,0,1:T(8,128)}, u32[]{:S(2)}) copy-start(f32[2,2,2,4,512]{3,4,2,0,1:T(8,128)} %copy.82) | copy-start | bytes 196612
  86.1 14.9 %copy-start.5 = (f32[2,2,2,4,512]{3,4,2,0,1:T(8,128)S(1)}, f32[2,2,2,4,512]{3,4,2,0,1:T(8,128)}, u32[]{:S(2)}) copy-start(f32[2,2,2,4,512]{3,4,2,0,1:T(8,128)} %copy.84) | copy-start | bytes 196612
  109.7 1.7 %copy-start.2 = (f32[2,2,2,128,512]{3,4,2,0,1:T(8,128)S(1)}, f32[2,2,2,128,512]{3,4,2,0,1:T(8,128)}, u32[]{:S(2)}) copy-start(f32[2,2,2,128,512]{3,4,2,0,1:T(8,128)} %copy-done) | copy-start | bytes 6291460
  112.5 1.3 copy-start.8
  116.9 1.5 %copy-start.12 = (f32[16,2,4]{2,1,0:T(2,128)S(1)}, f32[16,2,4]{2,1,0:T(2,128)}, u32[]{:S(2)}) copy-start(f32[16,2,4]{2,1,0:T(2,128)} %fusion.44) | copy-start | bytes 1540
  120.2 22.4 %all-to-all-start = ((f32[16,2,4096]{2,1,0:T(2,128)}), f32[16,2,4096]{2,1,0:T(2,128)S(1)}, u32[]{:S(2)}, u32[]{:S(2)}) async-start(f32[16,2,4096]{2,1,0:T(2,128)} %copy.89), calls=%async_computation | async-start | bytes 1048576 | tf_op jit(solution)/shard_map/all_to_all | solution.py:158
where the time goes:
time: 145 us; the launch traced here: 144 us
  other arithmetic  64.2 us (44%)
  local copies, waits for them, and re-layouts  38.7 us (27%)
  starting transfers between devices  19.6 us (14%)
  waiting for transfers between devices  14.2 us (10%)
  matrix products  6.78 us (5%)
    add x2, other arithmetic, derivatives(): first_z = first_z + FIRST_TERMS[offset - 1] * (upper_rows - lower_rows)  29.3 us
    add x2, other arithmetic, advance(): sine_tilt * sine_tilt * second_x + cosine * cosine * second_z  17.4 us
    all_to_all x1, waiting for transfers between devices, per_device(): lax.all_to_all(payload, 'slab', split_axis=0, concat_axis=0, tiled=True)  14.2 us
    another operation x2, other arithmetic  11 us
    ppermute x2, starting transfers between devices, padded(): before = lax.ppermute(last, axis, up)  8.92 us
    all_to_all x1, starting transfers between devices, per_device(): lax.all_to_all(payload, 'slab', split_axis=0, concat_axis=0, tiled=True)  8.15 us
    slice x3, local copies, waits for them, and re-layouts, padded(): last = lax.slice_in_dim(array, length - width, length, axis=dim)  7.17 us
    unnamed x35, local copies, waits for them, and re-layouts  7.06 us
  transfers between devices with their start and end apart: 5, of which 1 were waited for; matrix products, arithmetic and copies ran while one was open for 26% of the time, Pallas kernels for 0%

commit v1 on v0

v1 whole, which is shorter than its diff:
```python
import functools
import math

import jax
import jax.numpy as jnp
from jax import lax
from jax.experimental import pallas as pl
from jax.experimental.pallas import tpu as pltpu
from jax.sharding import PartitionSpec as P

MESH = pl.DeviceIdType.MESH
PAD = 16
REACH = 4
SECOND_TERMS = (-205.0 / 72.0, 8.0 / 5.0, -1.0 / 5.0, 8.0 / 315.0, -1.0 / 560.0)
FIRST_TERMS = (4.0 / 5.0, -1.0 / 5.0, 4.0 / 105.0, -1.0 / 280.0)


def sincos_turns(u):
    quarter = jnp.round(4.0 * u)
    theta = (u - 0.25 * quarter) * (2.0 * math.pi)
    sq = theta * theta
    sine = theta + theta * sq * (
        -1.0 / 6 + sq * (1.0 / 120 + sq * (-1.0 / 5040 + sq * (1.0 / 362880)))
    )
    cosine = 1.0 + sq * (-0.5 + sq * (1.0 / 24 + sq * (-1.0 / 720 + sq * (1.0 / 40320))))
    q = quarter.astype(jnp.int32)
    odd = (q & 1) == 1
    s = jnp.where(odd, cosine, sine)
    c = jnp.where(odd, sine, cosine)
    s = jnp.where((q & 2) == 2, -s, s)
    c = jnp.where(((q + 1) & 2) == 2, -c, c)
    return s, c


def band(distance, second):
    out = jnp.zeros(distance.shape, jnp.float32)
    if second:
        out = jnp.where(distance == 0, SECOND_TERMS[0], out)
    for offset in range(1, REACH + 1):
        weight = SECOND_TERMS[offset] if second else FIRST_TERMS[offset - 1]
        out = jnp.where(distance == offset, weight, out)
        out = jnp.where(distance == -offset, weight if second else -weight, out)
    return out


def iota(shape, dim):
    return lax.broadcasted_iota(jnp.int32, shape, dim)


def dot(a, b):
    return jnp.dot(a, b, preferred_element_type=jnp.float32)


def kernel(
    n,
    wav,
    courant,
    epsilon,
    delta,
    tilt,
    loc,
    counts,
    angle,
    out,
    state,
    c_in,
    e_in,
    d_in,
    t_in,
    ext1,
    ext2,
    ca,
    cb,
    cd,
    ce,
    cr,
    zmat,
    x2mat,
    x1mat,
    cos1,
    sin1,
    cos2,
    sin2,
    yre,
    yim,
    img,
    gath,
    in_sem,
    halo_send,
    halo_recv,
    ag_send,
    ag_recv,
):
    me = lax.axis_index("slab")
    _, _, shots, rows, cols = wav.shape
    patches = cols // rows
    bins = rows // 2
    angles = angle.shape[0]
    pairs = 2 * shots
    group = 2 * shots * patches
    half = group // 2
    block = out.shape[0]
    chunks = bins * angles // 128
    split = 8

    loads = []
    for j, (src, dst) in enumerate(
        (
            (wav.at[:, 0:2], state.at[:, 0:2]),
            (tilt, t_in),
            (epsilon, e_in),
            (delta, d_in),
            (courant, c_in),
            (wav.at[:, 2:4], state.at[:, 2:4]),
        )
    ):
        copy = pltpu.make_async_copy(src, dst, in_sem.at[j])
        copy.start()
        loads.append(copy)

    zero = jnp.zeros((2 * pairs, PAD, cols), jnp.bfloat16)
    for ext in (ext1, ext2):
        ext[:, 0:PAD, :] = zero
        ext[:, PAD + rows :, :] = zero

    barrier = pltpu.get_barrier_semaphore()
    for d in range(1, n):
        pl.semaphore_signal(
            barrier, inc=1, device_id={"slab": lax.rem(me + d, n)}, device_id_type=MESH
        )

    tall = rows + 2 * PAD
    reach = iota((rows, tall), 1) - PAD - iota((rows, tall), 0)
    zmat[0:rows] = band(reach, True).astype(jnp.bfloat16)
    zmat[rows:] = band(reach, False).astype(jnp.bfloat16)
    wide = iota((cols, cols), 0) - iota((cols, cols), 1)
    x2mat[...] = band(wide, True).astype(jnp.bfloat16)
    x1mat[...] = band(wide, False).astype(jnp.bfloat16)

    lanes = 2 * angles
    modulus = 16 * rows
    lane = iota((1, lanes), 1)
    slope = jnp.zeros((1, lanes), jnp.int32)
    for a in range(angles):
        slope = jnp.where(lane % angles == a, angle[a], slope)
    step = slope * iota((rows, lanes), 0)
    turn = jnp.where(iota((rows, lanes), 1) >= angles, modulus // 4, 0)
    scale = 1.0 / math.sqrt(rows)

    def phases(k, carry):
        j = jnp.bitwise_and(k * split * step, modulus - 1)
        s, c = sincos_turns(j.astype(jnp.float32) * (1.0 / modulus))
        cos1[k] = c
        sin1[k] = s
        j = jnp.bitwise_and(k * step + turn, modulus - 1)
        s, c = sincos_turns(j.astype(jnp.float32) * (1.0 / modulus))
        cos2[k] = c * scale
        sin2[k] = s * scale
        return carry

    lax.fori_loop(0, split, phases, 0)

    pl.semaphore_wait(barrier, n - 1)
    loads[0].wait()

    up = jnp.maximum(me - 1, 0)
    down = jnp.minimum(me + 1, n - 1)

    def halo(ext, step, i, upward):
        first = pl.ds(2 * i, 2)
        if upward:
            src = ext.at[first, PAD : 2 * PAD, :]
            dst = ext.at[first, PAD + rows : 2 * PAD + rows, :]
        else:
            src = ext.at[first, rows : PAD + rows, :]
            dst = ext.at[first, 0:PAD, :]
        way = 0 if upward else 1
        return pltpu.make_async_remote_copy(
            src_ref=src,
            dst_ref=dst,
            send_sem=halo_send.at[step, way, i],
            recv_sem=halo_recv.at[step, way, i],
            device_id={"slab": up if upward else down},
            device_id_type=MESH,
        )

    def send(ext, step, i):
        @pl.when(me > 0)
        def _():
            halo(ext, step, i, True).start()

        @pl.when(me < n - 1)
        def _():
            halo(ext, step, i, False).start()

    def receive(ext, step, i):
        @pl.when(me > 0)
        def _():
            halo(ext, step, i, False).wait_recv()

        @pl.when(me < n - 1)
        def _():
            halo(ext, step, i, True).wait_recv()

    def finish(ext, step, i):
        @pl.when(me > 0)
        def _():
            halo(ext, step, i, True).wait_send()

        @pl.when(me < n - 1)
        def _():
            halo(ext, step, i, False).wait_send()

    def convert(i, carry):
        f, s = i // shots, i % shots
        for w in range(2):
            ext1[2 * i + w, PAD : PAD + rows, :] = state[f, w, s].astype(jnp.bfloat16)
        send(ext1, 0, i)
        return carry

    lax.fori_loop(0, pairs, convert, 0)

    for copy in loads[1:5]:
        copy.wait()
    sine, cosine = sincos_turns(t_in[...] * (1.0 / math.pi))
    ca[...] = 0.5 - 0.5 * cosine
    cb[...] = 0.5 + 0.5 * cosine
    cd[...] = sine
    ce[...] = c_in[...] * (1.0 + 2.0 * e_in[...])
    cr[...] = c_in[...] * jnp.sqrt(1.0 + 2.0 * d_in[...])
    loads[5].wait()

    def terms(ext, field):
        z = dot(zmat[...], ext[field])
        xx = dot(ext[field, PAD : PAD + rows, :], x2mat[...])
        xz = dot(z[rows:].astype(jnp.bfloat16), x1mat[...])
        return xx, z[:rows], xz

    def first(i, carry):
        f, s = i // shots, i % shots
        receive(ext1, 0, i)
        xx, zz, xz = terms(ext1, 2 * i)
        across = cb[...] * xx + ca[...] * zz - cd[...] * xz
        xx, zz, xz = terms(ext1, 2 * i + 1)
        along = ca[...] * xx + cb[...] * zz + cd[...] * xz
        p = 2.0 * state[f, 0, s] - state[f, 2, s] + ce[...] * across + cr[...] * along
        q = 2.0 * state[f, 1, s] - state[f, 3, s] + cr[...] * across + c_in[...] * along
        state[f, 2, s] = p
        ext2[2 * i, PAD : PAD + rows, :] = p.astype(jnp.bfloat16)
        ext2[2 * i + 1, PAD : PAD + rows, :] = q.astype(jnp.bfloat16)
        send(ext2, 1, i)
        return carry

    lax.fori_loop(0, pairs, first, 0)

    kk = iota((rows, rows), 0)
    zz_ = iota((rows, rows), 1)
    turns = jnp.bitwise_and(jnp.where(kk >= bins, kk - bins, kk) * zz_, rows - 1)
    s_t, c_t = sincos_turns(turns.astype(jnp.float32) * (1.0 / rows))
    table = (jnp.where(kk >= bins, -s_t, c_t) * scale).astype(jnp.bfloat16)

    for i in range(pairs):
        f, s = i // shots, i % shots
        receive(ext2, 1, i)
        xx, zz, xz = terms(ext2, 2 * i)
        across = cb[...] * xx + ca[...] * zz - cd[...] * xz
        xx, zz, xz = terms(ext2, 2 * i + 1)
        along = ca[...] * xx + cb[...] * zz + cd[...] * xz
        p = 2.0 * state[f, 2, s] - state[f, 0, s] + ce[...] * across + cr[...] * along
        spectrum = dot(table, p.astype(jnp.bfloat16))
        for m in range(patches):
            part = spectrum[:, m * rows : (m + 1) * rows]
            slot = i * patches + m
            yre[pl.ds(slot, bins, stride=group), :] = part[:bins]
            yim[pl.ds(slot, bins, stride=group), :] = part[bins:]

    def stack(k):
        k1, k2 = k // split, k % split
        c1, s1, c2, s2 = cos1[k1], sin1[k1], cos2[k2], sin2[k2]
        weights = jnp.concatenate([c1 * c2 - s1 * s2, s1 * c2 + c1 * s2], axis=0)
        at = pl.ds(pl.multiple_of(k * group, group), group)
        data = jnp.concatenate([yre[at, :], yim[at, :]], axis=1)
        st = dot(data.astype(jnp.bfloat16), weights.astype(jnp.bfloat16))
        prod = st[:half] * st[half:]
        total = prod[:patches]
        for shot in range(1, shots):
            total = total + prod[shot * patches : (shot + 1) * patches]
        return total + pltpu.roll(total, angles, 1)

    side = iota((patches, lanes), 1)

    def images(t, carry):
        both = jnp.where(side < angles, stack(2 * t), stack(2 * t + 1))
        img[pl.ds(t, patches, stride=chunks), :] = both
        return carry

    lax.fori_loop(0, chunks, images, 0)

    live = iota((patches, chunks, lanes), 0) < counts[me]
    own = jnp.where(live, img[...].reshape(patches, chunks, lanes), 0.0)
    gath[pl.ds(me * patches, patches)] = own.astype(jnp.bfloat16)

    high = n // 4
    h, m, l = me // 4, (me // 2) % 2, me % 2
    sent = []

    def ident(a, b, c):
        return a * 4 + b * 2 + c

    def pass_on(b, target):
        at = gath.at[pl.ds(b * patches, patches)]
        copy = pltpu.make_async_remote_copy(
            src_ref=at,
            dst_ref=at,
            send_sem=ag_send.at[len(sent)],
            recv_sem=ag_recv.at[b],
            device_id={"slab": target},
            device_id_type=MESH,
        )
        copy.start()
        sent.append(copy)

    def arrive(b):
        at = gath.at[pl.ds(b * patches, patches)]
        pltpu.make_async_remote_copy(
            src_ref=at,
            dst_ref=at,
            send_sem=ag_send.at[0],
            recv_sem=ag_recv.at[b],
            device_id={"slab": ident(h, m, 1 - l)},
            device_id_type=MESH,
        ).wait_recv()

    mid, low = ident(h, 1 - m, l), ident(h, m, 1 - l)
    for d in range(1, high):
        pass_on(me, ident(lax.rem(h + d, high), m, l))
    pass_on(me, mid)
    pass_on(me, low)
    for d in range(1, high):
        b = ident(lax.rem(h + high - d, high), m, l)
        arrive(b)
        pass_on(b, mid)
        pass_on(b, low)
    for d in range(high):
        b = ident(lax.rem(h + high - d, high), 1 - m, l)
        arrive(b)
        pass_on(b, low)
    for d in range(high):
        a = lax.rem(h + high - d, high)
        arrive(ident(a, m, 1 - l))
        arrive(ident(a, 1 - m, 1 - l))

    for g in range(block):
        out[g] = gath[loc[me * block + g]].astype(jnp.float32)

    for copy in sent:
        copy.wait_send()
    for i in range(pairs):
        finish(ext1, 0, i)
        finish(ext2, 1, i)


def per_device(
    n, wavefields, courant, epsilon, anisotropy_delta, tilt_angle, loc_patch, slab_counts, angle_table
):
    _, _, shots, rows, cols = wavefields.shape
    patches = cols // rows
    bins = rows // 2
    angles = angle_table.shape[0]
    block = loc_patch.shape[0] // n
    chunks = bins * angles // 128
    pairs = 2 * shots
    group = pairs * patches
    high = n // 4
    f32, bf16 = jnp.float32, jnp.bfloat16
    vm = pltpu.VMEM
    plane = vm((rows, cols), f32)
    table = vm((8, rows, 2 * angles), f32)
    ext = vm((2 * pairs, rows + 2 * PAD, cols), bf16)
    hbm = pl.BlockSpec(memory_space=pl.ANY)
    smem = pl.BlockSpec(memory_space=pltpu.SMEM)
    result = pl.pallas_call(
        functools.partial(kernel, n),
        out_shape=jax.ShapeDtypeStruct((block, chunks, 128), f32),
        in_specs=[hbm] * 5 + [smem] * 3,
        out_specs=pl.BlockSpec(memory_space=pltpu.VMEM),
        scratch_shapes=[
            vm(wavefields.shape, f32),
            plane, plane, plane, plane,
            ext, ext,
            plane, plane, plane, plane, plane,
            vm((2 * rows, rows + 2 * PAD), bf16),
            vm((cols, cols), bf16),
            vm((cols, cols), bf16),
            table, table, table, table,
            vm((bins * group, rows), f32),
            vm((bins * group, rows), f32),
            vm((patches * chunks, 2 * angles), f32),
            vm((n * patches, chunks, 2 * angles), bf16),
            pltpu.SemaphoreType.DMA((6,)),
            pltpu.SemaphoreType.DMA((2, 2, pairs)),
            pltpu.SemaphoreType.DMA((2, 2, pairs)),
            pltpu.SemaphoreType.DMA((4 * high,)),
            pltpu.SemaphoreType.DMA((n,)),
        ],
        compiler_params=pltpu.CompilerParams(
            collective_id=0, has_side_effects=True, vmem_limit_bytes=48 * 1024 * 1024
        ),
        name="imaging",
    )(wavefields, courant, epsilon, anisotropy_delta, tilt_angle, loc_patch, slab_counts, angle_table)
    return result.reshape(block, chunks * 128)


def solution(mesh):
    return jax.shard_map(
        functools.partial(per_device, mesh.shape["slab"]),
        mesh=mesh,
        in_specs=(
            P(None, None, "groups", "slab", None),
            P("slab", None),
            P("slab", None),
            P("slab", None),
            P("slab", None),
            P(),
            P(),
            P(),
        ),
        out_specs=P(("groups", "slab"), None),
        check_vma=False,
    )
```

time: 145 us -> 41.8 us (0.29)
  other arithmetic: 64.2 us -> 0 us
  Pallas kernels: 0 us -> 32.7 us
  local copies, waits for them, and re-layouts: 38.7 us -> 8.83 us
  starting transfers between devices: 19.6 us -> 0 us
  waiting for transfers between devices: 14.2 us -> 0 us
  matrix products: 6.78 us -> 0 us
    add x8 -> x0, other arithmetic: 50.7 us -> none  [the longest x2 29.3 us: derivatives(): first_z = first_z + FIRST_TERMS[offset - 1] * (upper_rows - lower_rows)]
    pallas_call x0 -> x1, Pallas kernels: none -> 32.7 us  [per_device(): pl.pallas_call(functools.partial(kernel, n), out_shape=jax.ShapeDtypeStru...]
    slice x5 -> x0, local copies, waits for them, and re-layouts: 14.2 us -> none  [the longest x3 7.17 us: padded(): last = lax.slice_in_dim(array, length - width, length, axis=dim)]
    all_to_all x1 -> x0, waiting for transfers between devices: 14.2 us -> none  [per_device(): lax.all_to_all(payload, 'slab', split_axis=0, concat_axis=0, tiled=True)]
    ppermute x4 -> x0, starting transfers between devices: 11.5 us -> none  [the longest x2 8.92 us: padded(): before = lax.ppermute(last, axis, up)]
    another operation x2 -> x0, other arithmetic: 11 us -> none
    ppermute x4 -> x0, local copies, waits for them, and re-layouts: 9.6 us -> none  [the longest x2 4.88 us: padded(): before = lax.ppermute(last, axis, up)]
    all_to_all x1 -> x0, starting transfers between devices: 8.15 us -> none  [per_device(): lax.all_to_all(payload, 'slab', split_axis=0, concat_axis=0, tiled=True)]
  transfers between devices with their start and end apart: 5 -> 0, of which waited for: 1 -> 0; matrix products, arithmetic and copies ran while one was open for 26% -> 0% of each run, Pallas kernels for 0% -> 0%
where the time goes in v1:
time: 41.8 us; the launch traced here: 41.5 us
  Pallas kernels  32.7 us (78%)
  local copies, waits for them, and re-layouts  8.83 us (21%)
    pallas_call x1, Pallas kernels, per_device(): pl.pallas_call(functools.partial(kernel, n), out_shape=jax.ShapeDtypeStru...  32.7 us
    unnamed x17, local copies, waits for them, and re-layouts  8.83 us

profile of v1, /device:TPU:0, one launch (start us, length us, event | category | flops | bytes accessed | tf_op | source)
XLA Modules:
  0.0 41.5 jit_solution(12575798088079867707)
XLA Ops:
  0.0 0.0 copy-start
  0.0 2.2 %copy-done = f32[2,4,2,128,512]{4,3,2,1,0:T(8,128)S(1)} copy-done((f32[2,4,2,128,512]{4,3,2,1,0:T(8,128)S(1)}, f32[2,4,2,128,512]{4,3,2,1,0:T(8,128)}, u32[]{:S(2)}) %copy-start) | copy-done | bytes 4194328
  2.2 0.0 copy-start.1
  2.2 0.9 %copy-done.1 = f32[128,512]{1,0:T(8,128)S(1)} copy-done((f32[128,512]{1,0:T(8,128)S(1)}, f32[128,512]{1,0:T(8,128)}, u32[]{:S(2)}) %copy-start.1) | copy-done | bytes 262168
  3.1 0.0 copy-start.2
  3.1 0.9 %copy-done.2 = f32[128,512]{1,0:T(8,128)S(1)} copy-done((f32[128,512]{1,0:T(8,128)S(1)}, f32[128,512]{1,0:T(8,128)}, u32[]{:S(2)}) %copy-start.2) | copy-done | bytes 262168
  4.1 0.0 copy-start.3
  4.1 0.9 %copy-done.3 = f32[128,512]{1,0:T(8,128)S(1)} copy-done((f32[128,512]{1,0:T(8,128)S(1)}, f32[128,512]{1,0:T(8,128)}, u32[]{:S(2)}) %copy-start.3) | copy-done | bytes 262168
  5.0 0.0 copy-start.4
  5.0 0.9 %copy-done.4 = f32[128,512]{1,0:T(8,128)S(1)} copy-done((f32[128,512]{1,0:T(8,128)S(1)}, f32[128,512]{1,0:T(8,128)}, u32[]{:S(2)}) %copy-start.4) | copy-done | bytes 262168
  6.0 0.0 copy-start.5
  6.0 0.7 %copy-done.5 = s32[256]{0:T(256)S(1)} copy-done((s32[256]{0:T(256)S(1)}, s32[256]{0:T(256)}, u32[]{:S(2)}) %copy-start.5) | copy-done | bytes 1048
  6.7 0.0 copy-start.6
  6.7 0.7 %copy-done.6 = s32[16]{0:T(128)S(1)} copy-done((s32[16]{0:T(128)S(1)}, s32[16]{0:T(128)}, u32[]{:S(2)}) %copy-start.6) | copy-done | bytes 88
  7.3 0.0 copy-start.7
  7.3 0.7 %copy-done.7 = s32[64]{0:T(128)S(1)} copy-done((s32[64]{0:T(128)S(1)}, s32[64]{0:T(128)}, u32[]{:S(2)}) %copy-start.7) | copy-done | bytes 280
  8.0 32.7 %imaging.1 = f32[16,32,128]{2,1,0:T(8,128)S(1)} custom-call(f32[2,4,2,128,512]{4,3,2,1,0:T(8,128)S(1)} %copy-done, f32[128,512]{1,0:T(8,128)S(1)} %copy-done.1, f32[128,512]{1,0:T(8,128)S(1)} %copy-done.2, f32[128,512]{1,0:T(8,128)S(1)} %copy-done.3, f32[128,512]{1,0:T(8,128)S(1)} %copy-done.4, s32[256]{0:T(256)S(1)} %copy-done.5, s32[16]{0:T(128)S(1)} %copy-done.6, ...), custom_call_target="tpu_custom_call" | custom-call | tf_op jit(solution)/shard_map/imaging/pallas_call | solution.py:382
  40.7 0.9 %copy.11 = f32[2,8,32,128]{3,1,2,0:T(8,128)} copy(f32[2,8,32,128]{3,2,1,0:T(8,128)S(1)} %bitcast.4) | data formatting | bytes 524288
Async XLA Ops:
  0.0 2.2 %copy-start = (f32[2,4,2,128,512]{4,3,2,1,0:T(8,128)S(1)}, f32[2,4,2,128,512]{4,3,2,1,0:T(8,128)}, u32[]{:S(2)}) copy-start(f32[2,4,2,128,512]{4,3,2,1,0:T(8,128)} %wav.1) | copy-start | bytes 12582916
  2.2 0.9 %copy-start.1 = (f32[128,512]{1,0:T(8,128)S(1)}, f32[128,512]{1,0:T(8,128)}, u32[]{:S(2)}) copy-start(f32[128,512]{1,0:T(8,128)} %courant.1) | copy-start | bytes 786436
  3.1 0.9 %copy-start.2 = (f32[128,512]{1,0:T(8,128)S(1)}, f32[128,512]{1,0:T(8,128)}, u32[]{:S(2)}) copy-start(f32[128,512]{1,0:T(8,128)} %epsilon.1) | copy-start | bytes 786436
  4.1 0.9 %copy-start.3 = (f32[128,512]{1,0:T(8,128)S(1)}, f32[128,512]{1,0:T(8,128)}, u32[]{:S(2)}) copy-start(f32[128,512]{1,0:T(8,128)} %delta.1) | copy-start | bytes 786436
  5.0 0.9 %copy-start.4 = (f32[128,512]{1,0:T(8,128)S(1)}, f32[128,512]{1,0:T(8,128)}, u32[]{:S(2)}) copy-start(f32[128,512]{1,0:T(8,128)} %tilt.1) | copy-start | bytes 786436
  6.0 0.7 %copy-start.5 = (s32[256]{0:T(256)S(1)}, s32[256]{0:T(256)}, u32[]{:S(2)}) copy-start(s32[256]{0:T(256)} %loc.1) | copy-start | bytes 3076
  6.7 0.7 %copy-start.6 = (s32[16]{0:T(128)S(1)}, s32[16]{0:T(128)}, u32[]{:S(2)}) copy-start(s32[16]{0:T(128)} %counts.1) | copy-start | bytes 196
  7.3 0.7 %copy-start.7 = (s32[64]{0:T(128)S(1)}, s32[64]{0:T(128)}, u32[]{:S(2)}) copy-start(s32[64]{0:T(128)} %angle.1) | copy-start | bytes 772

commit v2 on v1

--- a/solution.py
+++ b/solution.py
@@ -33,11 +33,10 @@
 
 
 def band(distance, second):
+    taps = SECOND_TERMS[1:] if second else FIRST_TERMS
     out = jnp.zeros(distance.shape, jnp.float32)
-    if second:
-        out = jnp.where(distance == 0, SECOND_TERMS[0], out)
     for offset in range(1, REACH + 1):
-        weight = SECOND_TERMS[offset] if second else FIRST_TERMS[offset - 1]
+        weight = taps[offset - 1] / taps[0]
         out = jnp.where(distance == offset, weight, out)
         out = jnp.where(distance == -offset, weight if second else -weight, out)
     return out
@@ -223,12 +222,15 @@
     for copy in loads[1:5]:
         copy.wait()
     sine, cosine = sincos_turns(t_in[...] * (1.0 / math.pi))
-    ca[...] = 0.5 - 0.5 * cosine
-    cb[...] = 0.5 + 0.5 * cosine
-    cd[...] = sine
+    second_scale, first_scale = SECOND_TERMS[1], FIRST_TERMS[0]
+    ca[...] = (0.5 * second_scale) * (1.0 - cosine)
+    cb[...] = (0.5 * second_scale) * (1.0 + cosine)
+    cd[...] = (first_scale * first_scale) * sine
     ce[...] = c_in[...] * (1.0 + 2.0 * e_in[...])
     cr[...] = c_in[...] * jnp.sqrt(1.0 + 2.0 * d_in[...])
     loads[5].wait()
+
+    centre = SECOND_TERMS[0]
 
     def terms(ext, field):
         z = dot(zmat[...], ext[field])
@@ -240,12 +242,13 @@
         f, s = i // shots, i % shots
         receive(ext1, 0, i)
         xx, zz, xz = terms(ext1, 2 * i)
-        across = cb[...] * xx + ca[...] * zz - cd[...] * xz
+        across = cb[...] * xx + ca[...] * zz - cd[...] * xz + centre * state[f, 0, s]
         xx, zz, xz = terms(ext1, 2 * i + 1)
-        along = ca[...] * xx + cb[...] * zz + cd[...] * xz
+        along = ca[...] * xx + cb[...] * zz + cd[...] * xz + centre * state[f, 1, s]
         p = 2.0 * state[f, 0, s] - state[f, 2, s] + ce[...] * across + cr[...] * along
         q = 2.0 * state[f, 1, s] - state[f, 3, s] + cr[...] * across + c_in[...] * along
         state[f, 2, s] = p
+        state[f, 3, s] = q
         ext2[2 * i, PAD : PAD + rows, :] = p.astype(jnp.bfloat16)
         ext2[2 * i + 1, PAD : PAD + rows, :] = q.astype(jnp.bfloat16)
         send(ext2, 1, i)
@@ -257,17 +260,22 @@
     zz_ = iota((rows, rows), 1)
     turns = jnp.bitwise_and(jnp.where(kk >= bins, kk - bins, kk) * zz_, rows - 1)
     s_t, c_t = sincos_turns(turns.astype(jnp.float32) * (1.0 / rows))
-    table = (jnp.where(kk >= bins, -s_t, c_t) * scale).astype(jnp.bfloat16)
+    table = jnp.where(kk >= bins, -s_t, c_t) * scale
+    table_hi = table.astype(jnp.bfloat16)
+    table_lo = (table - table_hi.astype(jnp.float32)).astype(jnp.bfloat16)
+    table = jnp.concatenate([table_hi, table_hi], axis=1)
 
     for i in range(pairs):
         f, s = i // shots, i % shots
         receive(ext2, 1, i)
         xx, zz, xz = terms(ext2, 2 * i)
-        across = cb[...] * xx + ca[...] * zz - cd[...] * xz
+        across = cb[...] * xx + ca[...] * zz - cd[...] * xz + centre * state[f, 2, s]
         xx, zz, xz = terms(ext2, 2 * i + 1)
-        along = ca[...] * xx + cb[...] * zz + cd[...] * xz
+        along = ca[...] * xx + cb[...] * zz + cd[...] * xz + centre * state[f, 3, s]
         p = 2.0 * state[f, 2, s] - state[f, 0, s] + ce[...] * across + cr[...] * along
-        spectrum = dot(table, p.astype(jnp.bfloat16))
+        p_hi = p.astype(jnp.bfloat16)
+        p_lo = (p - p_hi.astype(jnp.float32)).astype(jnp.bfloat16)
+        spectrum = dot(table, jnp.concatenate([p_hi, p_lo], axis=0)) + dot(table_lo, p_hi)
         for m in range(patches):
             part = spectrum[:, m * rows : (m + 1) * rows]
             slot = i * patches + m
@@ -377,7 +385,7 @@
     plane = vm((rows, cols), f32)
     table = vm((8, rows, 2 * angles), f32)
     ext = vm((2 * pairs, rows + 2 * PAD, cols), bf16)
-    hbm = pl.BlockSpec(memory_space=pl.ANY)
+    hbm = pl.BlockSpec(memory_space=pltpu.HBM)
     smem = pl.BlockSpec(memory_space=pltpu.SMEM)
     result = pl.pallas_call(
         functools.partial(kernel, n),
@@ -404,7 +412,7 @@
             pltpu.SemaphoreType.DMA((n,)),
         ],
         compiler_params=pltpu.CompilerParams(
-            collective_id=0, has_side_effects=True, vmem_limit_bytes=48 * 1024 * 1024
+            collective_id=0, has_side_effects=True, vmem_limit_bytes=60 * 1024 * 1024
         ),
         name="imaging",
     )(wavefields, courant, epsilon, anisotropy_delta, tilt_angle, loc_patch, slab_counts, angle_table)

time: 41.8 us -> 35.6 us (0.85)
  local copies, waits for them, and re-layouts: 8.83 us -> 1.81 us
  Pallas kernels: 32.7 us -> 33.6 us
    unnamed x17 -> x1, local copies, waits for them, and re-layouts: 8.83 us -> 1.81 us
    pallas_call x1, Pallas kernels: 32.7 us -> 33.6 us  [per_device(): pl.pallas_call(functools.partial(kernel, n), out_shape=jax.ShapeDtypeStru...]
where the time goes in v2:
time: 35.6 us; the launch traced here: 35.4 us
  Pallas kernels  33.6 us (94%)
  local copies, waits for them, and re-layouts  1.81 us (5%)
    pallas_call x1, Pallas kernels, per_device(): pl.pallas_call(functools.partial(kernel, n), out_shape=jax.ShapeDtypeStru...  33.6 us
    unnamed x1, local copies, waits for them, and re-layouts  1.81 us

profile of v2, /device:TPU:0, one launch (start us, length us, event | category | flops | bytes accessed | tf_op | source)
XLA Modules:
  0.0 35.4 jit_solution(5609060199480935641)
XLA Ops:
  0.0 33.6 %imaging.1 = f32[16,32,128]{2,1,0:T(8,128)} custom-call(f32[2,4,2,128,512]{4,3,2,1,0:T(8,128)} %wav.1, f32[128,512]{1,0:T(8,128)} %courant.1, f32[128,512]{1,0:T(8,128)} %epsilon.1, f32[128,512]{1,0:T(8,128)} %delta.1, f32[128,512]{1,0:T(8,128)} %tilt.1, s32[256]{0:T(256)} %loc.1, s32[16]{0:T(128)} %counts.1, s32[64]{0:T(128)} %angle.1), custom_call_target="tpu_custom_call" | custom-call | tf_op jit(solution)/shard_map/imaging/pallas_call | solution.py:390
  33.6 1.8 %copy.11 = f32[2,8,32,128]{3,1,2,0:T(8,128)} copy(f32[2,8,32,128]{3,2,1,0:T(8,128)} %bitcast.4) | data formatting | bytes 524288

commit v3 on v2

--- a/solution.py
+++ b/solution.py
@@ -11,6 +11,7 @@
 MESH = pl.DeviceIdType.MESH
 PAD = 16
 REACH = 4
+LANES = 128
 SECOND_TERMS = (-205.0 / 72.0, 8.0 / 5.0, -1.0 / 5.0, 8.0 / 315.0, -1.0 / 560.0)
 FIRST_TERMS = (4.0 / 5.0, -1.0 / 5.0, 4.0 / 105.0, -1.0 / 280.0)
 
@@ -76,6 +77,11 @@
     zmat,
     x2mat,
     x1mat,
+    x2edge,
+    x1edge,
+    step_c,
+    step_s,
+    slant,
     cos1,
     sin1,
     cos2,
@@ -102,20 +108,27 @@
     chunks = bins * angles // 128
     split = 8
 
-    loads = []
-    for j, (src, dst) in enumerate(
-        (
-            (wav.at[:, 0:2], state.at[:, 0:2]),
-            (tilt, t_in),
-            (epsilon, e_in),
-            (delta, d_in),
-            (courant, c_in),
-            (wav.at[:, 2:4], state.at[:, 2:4]),
-        )
-    ):
+    def load(j, src, dst):
         copy = pltpu.make_async_copy(src, dst, in_sem.at[j])
         copy.start()
-        loads.append(copy)
+        return copy
+
+    def fields(i, first):
+        f, s = i // shots, i % shots
+        at = (f, pl.ds(first, 2), s)
+        return load(4 + 2 * i + first // 2, wav.at[at], state.at[at])
+
+    now, before = [fields(0, 0)], []
+    coefs = [
+        load(j, src, dst)
+        for j, (src, dst) in enumerate(
+            ((tilt, t_in), (epsilon, e_in), (delta, d_in), (courant, c_in))
+        )
+    ]
+    for i in range(1, pairs):
+        now.append(fields(i, 0))
+        before.append(fields(i - 1, 2))
+    before.append(fields(pairs - 1, 2))
 
     zero = jnp.zeros((2 * pairs, PAD, cols), jnp.bfloat16)
     for ext in (ext1, ext2):
@@ -132,9 +145,17 @@
     reach = iota((rows, tall), 1) - PAD - iota((rows, tall), 0)
     zmat[0:rows] = band(reach, True).astype(jnp.bfloat16)
     zmat[rows:] = band(reach, False).astype(jnp.bfloat16)
-    wide = iota((cols, cols), 0) - iota((cols, cols), 1)
-    x2mat[...] = band(wide, True).astype(jnp.bfloat16)
-    x1mat[...] = band(wide, False).astype(jnp.bfloat16)
+    apart = iota((LANES, LANES), 0) - iota((LANES, LANES), 1)
+    for mat, edge, second in ((x2mat, x2edge, True), (x1mat, x1edge, False)):
+        here = band(apart, second).astype(jnp.bfloat16)
+        left = band(apart - LANES, second).astype(jnp.bfloat16)
+        right = band(apart + LANES, second).astype(jnp.bfloat16)
+        mat[0:LANES, 0:LANES] = here
+        mat[LANES:, LANES:] = here
+        mat[0:LANES, LANES:] = left
+        mat[LANES:, 0:LANES] = right
+        edge[0] = left
+        edge[1] = right
 
     lanes = 2 * angles
     modulus = 16 * rows
@@ -143,24 +164,38 @@
     for a in range(angles):
         slope = jnp.where(lane % angles == a, angle[a], slope)
     step = slope * iota((rows, lanes), 0)
-    turn = jnp.where(iota((rows, lanes), 1) >= angles, modulus // 4, 0)
     scale = 1.0 / math.sqrt(rows)
 
+    def phase(j):
+        j = jnp.bitwise_and(j, modulus - 1)
+        return sincos_turns(j.astype(jnp.float32) * (1.0 / modulus))
+
+    one = jnp.ones((rows, lanes), jnp.float32)
+    sin1[0], cos1[0] = 0.0 * one, one
+    fine_s, fine_c = phase(step)
+    coarse_s, coarse_c = phase(split * step)
+    first_half = iota((rows, lanes), 1) < angles
+    sin2[0] = jnp.where(first_half, 0.0, scale)
+    cos2[0] = jnp.where(first_half, scale, 0.0)
+    sin1[1], cos1[1] = coarse_s, coarse_c
+    sin2[1] = jnp.where(first_half, fine_s, fine_c) * scale
+    cos2[1] = jnp.where(first_half, fine_c, -fine_s) * scale
+
     def phases(k, carry):
-        j = jnp.bitwise_and(k * split * step, modulus - 1)
-        s, c = sincos_turns(j.astype(jnp.float32) * (1.0 / modulus))
-        cos1[k] = c
-        sin1[k] = s
-        j = jnp.bitwise_and(k * step + turn, modulus - 1)
-        s, c = sincos_turns(j.astype(jnp.float32) * (1.0 / modulus))
-        cos2[k] = c * scale
-        sin2[k] = s * scale
+        c, s = cos1[k], sin1[k]
+        cos1[k + 1] = c * cos1[1] - s * sin1[1]
+        sin1[k + 1] = s * cos1[1] + c * sin1[1]
+        c, s = cos2[k], sin2[k]
+        fc, fs = step_c[...], step_s[...]
+        cos2[k + 1] = c * fc - s * fs
+        sin2[k + 1] = s * fc + c * fs
         return carry
 
-    lax.fori_loop(0, split, phases, 0)
+    step_c[...] = fine_c
+    step_s[...] = fine_s
+    lax.fori_loop(1, split - 1, phases, 0)
 
     pl.semaphore_wait(barrier, n - 1)
-    loads[0].wait()
 
     up = jnp.maximum(me - 1, 0)
     down = jnp.minimum(me + 1, n - 1)
@@ -210,16 +245,16 @@
         def _():
             halo(ext, step, i, False).wait_send()
 
-    def convert(i, carry):
+    def convert(i):
         f, s = i // shots, i % shots
+        now[i].wait()
         for w in range(2):
             ext1[2 * i + w, PAD : PAD + rows, :] = state[f, w, s].astype(jnp.bfloat16)
         send(ext1, 0, i)
-        return carry
-
-    lax.fori_loop(0, pairs, convert, 0)
-
-    for copy in loads[1:5]:
+
+    convert(0)
+
+    for copy in coefs:
         copy.wait()
     sine, cosine = sincos_turns(t_in[...] * (1.0 / math.pi))
     second_scale, first_scale = SECOND_TERMS[1], FIRST_TERMS[0]
@@ -228,33 +263,63 @@
     cd[...] = (first_scale * first_scale) * sine
     ce[...] = c_in[...] * (1.0 + 2.0 * e_in[...])
     cr[...] = c_in[...] * jnp.sqrt(1.0 + 2.0 * d_in[...])
-    loads[5].wait()
+
+    def slants(k1, carry):
+        for k2 in range(split):
+            k = k1 * split + k2
+            for r in range(0, rows, 32):
+                at = pl.ds(r, 32)
+                c1, s1 = cos1[k1, at], sin1[k1, at]
+                c2, s2 = cos2[k2, at], sin2[k2, at]
+                slant[k, at, :] = (c1 * c2 - s1 * s2).astype(jnp.bfloat16)
+                slant[k, pl.ds(rows + r, 32), :] = (s1 * c2 + c1 * s2).astype(jnp.bfloat16)
+        return carry
+
+    lax.fori_loop(0, bins // split, slants, 0)
 
     centre = SECOND_TERMS[0]
 
-    def terms(ext, field):
-        z = dot(zmat[...], ext[field])
-        xx = dot(ext[field, PAD : PAD + rows, :], x2mat[...])
-        xz = dot(z[rows:].astype(jnp.bfloat16), x1mat[...])
-        return xx, z[:rows], xz
-
-    def first(i, carry):
+    wide = 2 * LANES
+
+    def along_x(x, mat, edge):
+        pieces = []
+        for c in range(0, cols, wide):
+            y = dot(x[:, c : c + wide], mat[...])
+            low, top = y[:, :LANES], y[:, LANES:]
+            if c > 0:
+                low = low + dot(x[:, c - LANES : c], edge[0])
+            if c + wide < cols:
+                top = top + dot(x[:, c + wide : c + wide + LANES], edge[1])
+            pieces += [low, top]
+        return jnp.concatenate(pieces, axis=1)
+
+    def terms(ext, i, p, q):
+        zp = dot(zmat[...], ext[2 * i])
+        zq = dot(zmat[...], ext[2 * i + 1])
+        both = ext[2 * i : 2 * i + 2, PAD : PAD + rows, :].reshape(2 * rows, cols)
+        xx = along_x(both, x2mat, x2edge)
+        mixed = jnp.concatenate([zp[rows:], zq[rows:]], axis=0).astype(jnp.bfloat16)
+        xz = along_x(mixed, x1mat, x1edge)
+        a, b, d = ca[...], cb[...], cd[...]
+        across = b * xx[:rows] + a * zp[:rows] - d * xz[:rows] + centre * p
+        along = a * xx[rows:] + b * zq[:rows] + d * xz[rows:] + centre * q
+        return across, along
+
+    for i in range(pairs):
         f, s = i // shots, i % shots
+        if i + 1 < pairs:
+            convert(i + 1)
+        before[i].wait()
         receive(ext1, 0, i)
-        xx, zz, xz = terms(ext1, 2 * i)
-        across = cb[...] * xx + ca[...] * zz - cd[...] * xz + centre * state[f, 0, s]
-        xx, zz, xz = terms(ext1, 2 * i + 1)
-        along = ca[...] * xx + cb[...] * zz + cd[...] * xz + centre * state[f, 1, s]
-        p = 2.0 * state[f, 0, s] - state[f, 2, s] + ce[...] * across + cr[...] * along
-        q = 2.0 * state[f, 1, s] - state[f, 3, s] + cr[...] * across + c_in[...] * along
+        p0, q0 = state[f, 0, s], state[f, 1, s]
+        across, along = terms(ext1, i, p0, q0)
+        p = 2.0 * p0 - state[f, 2, s] + ce[...] * across + cr[...] * along
+        q = 2.0 * q0 - state[f, 3, s] + cr[...] * across + c_in[...] * along
         state[f, 2, s] = p
         state[f, 3, s] = q
         ext2[2 * i, PAD : PAD + rows, :] = p.astype(jnp.bfloat16)
         ext2[2 * i + 1, PAD : PAD + rows, :] = q.astype(jnp.bfloat16)
         send(ext2, 1, i)
-        return carry
-
-    lax.fori_loop(0, pairs, first, 0)
 
     kk = iota((rows, rows), 0)
     zz_ = iota((rows, rows), 1)
@@ -268,11 +333,9 @@
     for i in range(pairs):
         f, s = i // shots, i % shots
         receive(ext2, 1, i)
-        xx, zz, xz = terms(ext2, 2 * i)
-        across = cb[...] * xx + ca[...] * zz - cd[...] * xz + centre * state[f, 2, s]
-        xx, zz, xz = terms(ext2, 2 * i + 1)
-        along = ca[...] * xx + cb[...] * zz + cd[...] * xz + centre * state[f, 3, s]
-        p = 2.0 * state[f, 2, s] - state[f, 0, s] + ce[...] * across + cr[...] * along
+        p1 = state[f, 2, s]
+        across, along = terms(ext2, i, p1, state[f, 3, s])
+        p = 2.0 * p1 - state[f, 0, s] + ce[...] * across + cr[...] * along
         p_hi = p.astype(jnp.bfloat16)
         p_lo = (p - p_hi.astype(jnp.float32)).astype(jnp.bfloat16)
         spectrum = dot(table, jnp.concatenate([p_hi, p_lo], axis=0)) + dot(table_lo, p_hi)
@@ -283,30 +346,34 @@
             yim[pl.ds(slot, bins, stride=group), :] = part[bins:]
 
     def stack(k):
-        k1, k2 = k // split, k % split
-        c1, s1, c2, s2 = cos1[k1], sin1[k1], cos2[k2], sin2[k2]
-        weights = jnp.concatenate([c1 * c2 - s1 * s2, s1 * c2 + c1 * s2], axis=0)
         at = pl.ds(pl.multiple_of(k * group, group), group)
         data = jnp.concatenate([yre[at, :], yim[at, :]], axis=1)
-        st = dot(data.astype(jnp.bfloat16), weights.astype(jnp.bfloat16))
+        st = dot(data.astype(jnp.bfloat16), slant[k])
         prod = st[:half] * st[half:]
         total = prod[:patches]
         for shot in range(1, shots):
             total = total + prod[shot * patches : (shot + 1) * patches]
-        return total + pltpu.roll(total, angles, 1)
-
-    side = iota((patches, lanes), 1)
-
-    def images(t, carry):
-        both = jnp.where(side < angles, stack(2 * t), stack(2 * t + 1))
-        img[pl.ds(t, patches, stride=chunks), :] = both
+        return total
+
+    side = iota((patches, lanes), 1) < angles
+    unroll = 4
+
+    def images(j, carry):
+        for v in range(unroll):
+            t = j * unroll + v
+            even, odd = stack(2 * t), stack(2 * t + 1)
+            keep = jnp.where(side, even, odd)
+            give = jnp.where(side, odd, even)
+            img[pl.ds(t, patches, stride=chunks), :] = keep + pltpu.roll(give, angles, 1)
         return carry
 
-    lax.fori_loop(0, chunks, images, 0)
-
-    live = iota((patches, chunks, lanes), 0) < counts[me]
-    own = jnp.where(live, img[...].reshape(patches, chunks, lanes), 0.0)
-    gath[pl.ds(me * patches, patches)] = own.astype(jnp.bfloat16)
+    live = iota((patches, chunks // 2, lanes), 0) < counts[me]
+
+    def finish_half(w):
+        per = chunks // (2 * unroll)
+        lax.fori_loop(w * per, (w + 1) * per, images, 0)
+        own = jnp.where(live, img[...].reshape(patches, chunks, lanes)[:, w * (chunks // 2) : (w + 1) * (chunks // 2)], 0.0)
+        gath[pl.ds(me * patches, patches), w] = own.astype(jnp.bfloat16)
 
     high = n // 4
     h, m, l = me // 4, (me // 2) % 2, me % 2
@@ -315,51 +382,61 @@
     def ident(a, b, c):
         return a * 4 + b * 2 + c
 
-    def pass_on(b, target):
-        at = gath.at[pl.ds(b * patches, patches)]
+    def pass_on(b, w, target):
+        at = gath.at[pl.ds(b * patches, patches), w]
         copy = pltpu.make_async_remote_copy(
             src_ref=at,
             dst_ref=at,
             send_sem=ag_send.at[len(sent)],
-            recv_sem=ag_recv.at[b],
+            recv_sem=ag_recv.at[w, b],
             device_id={"slab": target},
             device_id_type=MESH,
         )
         copy.start()
         sent.append(copy)
 
-    def arrive(b):
-        at = gath.at[pl.ds(b * patches, patches)]
+    mid, low = ident(h, 1 - m, l), ident(h, m, 1 - l)
+
+    def arrive(b, w):
+        at = gath.at[pl.ds(b * patches, patches), w]
         pltpu.make_async_remote_copy(
             src_ref=at,
             dst_ref=at,
             send_sem=ag_send.at[0],
-            recv_sem=ag_recv.at[b],
-            device_id={"slab": ident(h, m, 1 - l)},
+            recv_sem=ag_recv.at[w, b],
+            device_id={"slab": low},
             device_id_type=MESH,
         ).wait_recv()
 
-    mid, low = ident(h, 1 - m, l), ident(h, m, 1 - l)
-    for d in range(1, high):
-        pass_on(me, ident(lax.rem(h + d, high), m, l))
-    pass_on(me, mid)
-    pass_on(me, low)
-    for d in range(1, high):
-        b = ident(lax.rem(h + high - d, high), m, l)
-        arrive(b)
-        pass_on(b, mid)
-        pass_on(b, low)
-    for d in range(high):
-        b = ident(lax.rem(h + high - d, high), 1 - m, l)
-        arrive(b)
-        pass_on(b, low)
-    for d in range(high):
-        a = lax.rem(h + high - d, high)
-        arrive(ident(a, m, 1 - l))
-        arrive(ident(a, 1 - m, 1 - l))
+    for w in range(2):
+        finish_half(w)
+        pass_on(me, w, mid)
+        for d in range(1, high):
+            pass_on(me, w, ident(lax.rem(h + d, high), m, l))
+        pass_on(me, w, low)
+    for w in range(2):
+        b = ident(h, 1 - m, l)
+        arrive(b, w)
+        pass_on(b, w, low)
+        for d in range(1, high):
+            a = lax.rem(h + high - d, high)
+            b = ident(a, m, l)
+            arrive(b, w)
+            pass_on(b, w, mid)
+            pass_on(b, w, low)
+    for w in range(2):
+        for d in range(1, high):
+            b = ident(lax.rem(h + high - d, high), 1 - m, l)
+            arrive(b, w)
+            pass_on(b, w, low)
+    for w in range(2):
+        for d in range(high):
+            a = lax.rem(h + high - d, high)
+            arrive(ident(a, m, 1 - l), w)
+            arrive(ident(a, 1 - m, 1 - l), w)
 
     for g in range(block):
-        out[g] = gath[loc[me * block + g]].astype(jnp.float32)
+        out[g] = gath[loc[me * block + g]].astype(jnp.float32).reshape(chunks, lanes)
 
     for copy in sent:
         copy.wait_send()
@@ -398,18 +475,23 @@
             ext, ext,
             plane, plane, plane, plane, plane,
             vm((2 * rows, rows + 2 * PAD), bf16),
-            vm((cols, cols), bf16),
-            vm((cols, cols), bf16),
+            vm((2 * LANES, 2 * LANES), bf16),
+            vm((2 * LANES, 2 * LANES), bf16),
+            vm((2, LANES, LANES), bf16),
+            vm((2, LANES, LANES), bf16),
+            vm((rows, 2 * angles), f32),
+            vm((rows, 2 * angles), f32),
+            vm((bins, 2 * rows, 2 * angles), bf16),
             table, table, table, table,
             vm((bins * group, rows), f32),
             vm((bins * group, rows), f32),
             vm((patches * chunks, 2 * angles), f32),
-            vm((n * patches, chunks, 2 * angles), bf16),
-            pltpu.SemaphoreType.DMA((6,)),
+            vm((n * patches, 2, chunks // 2, 2 * angles), bf16),
+            pltpu.SemaphoreType.DMA((4 + 2 * pairs,)),
             pltpu.SemaphoreType.DMA((2, 2, pairs)),
             pltpu.SemaphoreType.DMA((2, 2, pairs)),
-            pltpu.SemaphoreType.DMA((4 * high,)),
-            pltpu.SemaphoreType.DMA((n,)),
+            pltpu.SemaphoreType.DMA((8 * high,)),
+            pltpu.SemaphoreType.DMA((2, n)),
         ],
         compiler_params=pltpu.CompilerParams(
             collective_id=0, has_side_effects=True, vmem_limit_bytes=60 * 1024 * 1024

time: 35.6 us -> 31.3 us (0.88)
  Pallas kernels: 33.6 us -> 29.4 us
    pallas_call x1, Pallas kernels: 33.6 us -> 29.4 us  [per_device(): pl.pallas_call(functools.partial(kernel, n), out_shape=jax.ShapeDtypeStru...]
where the time goes in v3:
time: 31.3 us; the launch traced here: 31.2 us
  Pallas kernels  29.4 us (94%)
  local copies, waits for them, and re-layouts  1.81 us (6%)
    pallas_call x1, Pallas kernels, per_device(): pl.pallas_call(functools.partial(kernel, n), out_shape=jax.ShapeDtypeStru...  29.4 us
    unnamed x1, local copies, waits for them, and re-layouts  1.81 us

profile of v3, /device:TPU:0, one launch (start us, length us, event | category | flops | bytes accessed | tf_op | source)
XLA Modules:
  0.0 31.2 jit_solution(14768865619838521806)
XLA Ops:
  0.0 29.4 %imaging.1 = f32[16,32,128]{2,1,0:T(8,128)} custom-call(f32[2,4,2,128,512]{4,3,2,1,0:T(8,128)} %wav.1, f32[128,512]{1,0:T(8,128)} %courant.1, f32[128,512]{1,0:T(8,128)} %epsilon.1, f32[128,512]{1,0:T(8,128)} %delta.1, f32[128,512]{1,0:T(8,128)} %tilt.1, s32[256]{0:T(256)} %loc.1, s32[16]{0:T(128)} %counts.1, s32[64]{0:T(128)} %angle.1), custom_call_target="tpu_custom_call" | custom-call | tf_op jit(solution)/shard_map/imaging/pallas_call | solution.py:467
  29.4 1.8 %copy.11 = f32[2,8,32,128]{3,1,2,0:T(8,128)} copy(f32[2,8,32,128]{3,2,1,0:T(8,128)} %bitcast.4) | data formatting | bytes 524288

commit v4 on v3

--- a/solution.py
+++ b/solution.py
@@ -69,6 +69,8 @@
     t_in,
     ext1,
     ext2,
+    edges,
+    halos,
     ca,
     cb,
     cd,
@@ -118,22 +120,16 @@
         at = (f, pl.ds(first, 2), s)
         return load(4 + 2 * i + first // 2, wav.at[at], state.at[at])
 
-    now, before = [fields(0, 0)], []
+    now = [fields(i, 0) for i in range(pairs)]
     coefs = [
         load(j, src, dst)
         for j, (src, dst) in enumerate(
             ((tilt, t_in), (epsilon, e_in), (delta, d_in), (courant, c_in))
         )
     ]
-    for i in range(1, pairs):
-        now.append(fields(i, 0))
-        before.append(fields(i - 1, 2))
-    before.append(fields(pairs - 1, 2))
-
-    zero = jnp.zeros((2 * pairs, PAD, cols), jnp.bfloat16)
-    for ext in (ext1, ext2):
-        ext[:, 0:PAD, :] = zero
-        ext[:, PAD + rows :, :] = zero
+    before = [fields(i, 2) for i in range(pairs)]
+
+    halos[...] = jnp.zeros(halos.shape, jnp.bfloat16)
 
     barrier = pltpu.get_barrier_semaphore()
     for d in range(1, n):
@@ -142,9 +138,15 @@
         )
 
     tall = rows + 2 * PAD
-    reach = iota((rows, tall), 1) - PAD - iota((rows, tall), 0)
-    zmat[0:rows] = band(reach, True).astype(jnp.bfloat16)
-    zmat[rows:] = band(reach, False).astype(jnp.bfloat16)
+    col = iota((rows, tall), 1)
+    for w in range(2):
+        source = jnp.where(col < PAD, col - 8 * w - 8, col - PAD)
+        source = jnp.where(col >= PAD + rows, source - 8 * w, source)
+        strange = (col < PAD) & (col // 8 != w)
+        strange |= (col >= PAD + rows) & ((col - PAD - rows) // 8 != w)
+        reach = jnp.where(strange, rows, source - iota((rows, tall), 0))
+        zmat[w, 0:rows] = band(reach, True).astype(jnp.bfloat16)
+        zmat[w, rows:] = band(reach, False).astype(jnp.bfloat16)
     apart = iota((LANES, LANES), 0) - iota((LANES, LANES), 1)
     for mat, edge, second in ((x2mat, x2edge, True), (x1mat, x1edge, False)):
         here = band(apart, second).astype(jnp.bfloat16)
@@ -200,59 +202,61 @@
     up = jnp.maximum(me - 1, 0)
     down = jnp.minimum(me + 1, n - 1)
 
-    def halo(ext, step, i, upward):
-        first = pl.ds(2 * i, 2)
-        if upward:
-            src = ext.at[first, PAD : 2 * PAD, :]
-            dst = ext.at[first, PAD + rows : 2 * PAD + rows, :]
-        else:
-            src = ext.at[first, rows : PAD + rows, :]
-            dst = ext.at[first, 0:PAD, :]
+    def halo(step, i, upward):
         way = 0 if upward else 1
         return pltpu.make_async_remote_copy(
-            src_ref=src,
-            dst_ref=dst,
+            src_ref=edges.at[step, i, way],
+            dst_ref=halos.at[step, i, way],
             send_sem=halo_send.at[step, way, i],
             recv_sem=halo_recv.at[step, way, i],
             device_id={"slab": up if upward else down},
             device_id_type=MESH,
         )
 
-    def send(ext, step, i):
+    def put_edges(step, i, p, q):
+        for way, cut in ((0, slice(0, 8)), (1, slice(rows - 8, rows))):
+            both = jnp.concatenate([p[cut], q[cut]], axis=0)
+            edges[step, i, way] = both.astype(jnp.bfloat16)
+
+    def send(step, i):
         @pl.when(me > 0)
         def _():
-            halo(ext, step, i, True).start()
+            halo(step, i, True).start()
 
         @pl.when(me < n - 1)
         def _():
-            halo(ext, step, i, False).start()
-
-    def receive(ext, step, i):
+            halo(step, i, False).start()
+
+    def receive(step, i):
         @pl.when(me > 0)
         def _():
-            halo(ext, step, i, False).wait_recv()
+            halo(step, i, False).wait_recv()
 
         @pl.when(me < n - 1)
         def _():
-            halo(ext, step, i, True).wait_recv()
-
-    def finish(ext, step, i):
+            halo(step, i, True).wait_recv()
+
+    def finish(step, i):
         @pl.when(me > 0)
         def _():
-            halo(ext, step, i, True).wait_send()
+            halo(step, i, True).wait_send()
 
         @pl.when(me < n - 1)
         def _():
-            halo(ext, step, i, False).wait_send()
+            halo(step, i, False).wait_send()
 
     def convert(i):
         f, s = i // shots, i % shots
+        for w in range(2):
+            ext1[2 * i + w] = state[f, w, s].astype(jnp.bfloat16)
+
+    for i in range(pairs):
+        f, s = i // shots, i % shots
         now[i].wait()
-        for w in range(2):
-            ext1[2 * i + w, PAD : PAD + rows, :] = state[f, w, s].astype(jnp.bfloat16)
-        send(ext1, 0, i)
-
-    convert(0)
+        put_edges(0, i, state[f, 0, s], state[f, 1, s])
+        send(0, i)
+    for i in range(pairs):
+        convert(i)
 
     for copy in coefs:
         copy.wait()
@@ -293,10 +297,11 @@
             pieces += [low, top]
         return jnp.concatenate(pieces, axis=1)
 
-    def terms(ext, i, p, q):
-        zp = dot(zmat[...], ext[2 * i])
-        zq = dot(zmat[...], ext[2 * i + 1])
-        both = ext[2 * i : 2 * i + 2, PAD : PAD + rows, :].reshape(2 * rows, cols)
+    def terms(ext, step, i, p, q):
+        above, below = halos[step, i, 1], halos[step, i, 0]
+        zp = dot(zmat[0], jnp.concatenate([above, ext[2 * i], below], axis=0))
+        zq = dot(zmat[1], jnp.concatenate([above, ext[2 * i + 1], below], axis=0))
+        both = ext[2 * i : 2 * i + 2].reshape(2 * rows, cols)
         xx = along_x(both, x2mat, x2edge)
         mixed = jnp.concatenate([zp[rows:], zq[rows:]], axis=0).astype(jnp.bfloat16)
         xz = along_x(mixed, x1mat, x1edge)
@@ -307,19 +312,18 @@
 
     for i in range(pairs):
         f, s = i // shots, i % shots
-        if i + 1 < pairs:
-            convert(i + 1)
         before[i].wait()
-        receive(ext1, 0, i)
+        receive(0, i)
         p0, q0 = state[f, 0, s], state[f, 1, s]
-        across, along = terms(ext1, i, p0, q0)
+        across, along = terms(ext1, 0, i, p0, q0)
         p = 2.0 * p0 - state[f, 2, s] + ce[...] * across + cr[...] * along
         q = 2.0 * q0 - state[f, 3, s] + cr[...] * across + c_in[...] * along
         state[f, 2, s] = p
         state[f, 3, s] = q
-        ext2[2 * i, PAD : PAD + rows, :] = p.astype(jnp.bfloat16)
-        ext2[2 * i + 1, PAD : PAD + rows, :] = q.astype(jnp.bfloat16)
-        send(ext2, 1, i)
+        put_edges(1, i, p, q)
+        ext2[2 * i] = p.astype(jnp.bfloat16)
+        ext2[2 * i + 1] = q.astype(jnp.bfloat16)
+        send(1, i)
 
     kk = iota((rows, rows), 0)
     zz_ = iota((rows, rows), 1)
@@ -332,9 +336,9 @@
 
     for i in range(pairs):
         f, s = i // shots, i % shots
-        receive(ext2, 1, i)
+        receive(1, i)
         p1 = state[f, 2, s]
-        across, along = terms(ext2, i, p1, state[f, 3, s])
+        across, along = terms(ext2, 1, i, p1, state[f, 3, s])
         p = 2.0 * p1 - state[f, 0, s] + ce[...] * across + cr[...] * along
         p_hi = p.astype(jnp.bfloat16)
         p_lo = (p - p_hi.astype(jnp.float32)).astype(jnp.bfloat16)
@@ -441,8 +445,8 @@
     for copy in sent:
         copy.wait_send()
     for i in range(pairs):
-        finish(ext1, 0, i)
-        finish(ext2, 1, i)
+        finish(0, i)
+        finish(1, i)
 
 
 def per_device(
@@ -461,7 +465,8 @@
     vm = pltpu.VMEM
     plane = vm((rows, cols), f32)
     table = vm((8, rows, 2 * angles), f32)
-    ext = vm((2 * pairs, rows + 2 * PAD, cols), bf16)
+    ext = vm((2 * pairs, rows, cols), bf16)
+    rims = vm((2, pairs, 2, PAD, cols), bf16)
     hbm = pl.BlockSpec(memory_space=pltpu.HBM)
     smem = pl.BlockSpec(memory_space=pltpu.SMEM)
     result = pl.pallas_call(
@@ -472,9 +477,9 @@
         scratch_shapes=[
             vm(wavefields.shape, f32),
             plane, plane, plane, plane,
-            ext, ext,
+            ext, ext, rims, rims,
             plane, plane, plane, plane, plane,
-            vm((2 * rows, rows + 2 * PAD), bf16),
+            vm((2, 2 * rows, rows + 2 * PAD), bf16),
             vm((2 * LANES, 2 * LANES), bf16),
             vm((2 * LANES, 2 * LANES), bf16),
             vm((2, LANES, LANES), bf16),

time: 31.3 us -> 28 us (0.89)
  Pallas kernels: 29.4 us -> 26.1 us
    pallas_call x1, Pallas kernels: 29.4 us -> 26.1 us  [per_device(): pl.pallas_call(functools.partial(kernel, n), out_shape=jax.ShapeDtypeStru...]
where the time goes in v4:
time: 28 us; the launch traced here: 27.9 us
  Pallas kernels  26.1 us (93%)
  local copies, waits for them, and re-layouts  1.81 us (6%)
    pallas_call x1, Pallas kernels, per_device(): pl.pallas_call(functools.partial(kernel, n), out_shape=jax.ShapeDtypeStru...  26.1 us
    unnamed x1, local copies, waits for them, and re-layouts  1.81 us

profile of v4, /device:TPU:0, one launch (start us, length us, event | category | flops | bytes accessed | tf_op | source)
XLA Modules:
  0.0 27.9 jit_solution(3884844096151284311)
XLA Ops:
  0.0 26.1 %imaging.1 = f32[16,32,128]{2,1,0:T(8,128)} custom-call(f32[2,4,2,128,512]{4,3,2,1,0:T(8,128)} %wav.1, f32[128,512]{1,0:T(8,128)} %courant.1, f32[128,512]{1,0:T(8,128)} %epsilon.1, f32[128,512]{1,0:T(8,128)} %delta.1, f32[128,512]{1,0:T(8,128)} %tilt.1, s32[256]{0:T(256)} %loc.1, s32[16]{0:T(128)} %counts.1, s32[64]{0:T(128)} %angle.1), custom_call_target="tpu_custom_call" | custom-call | tf_op jit(solution)/shard_map/imaging/pallas_call | solution.py:472
  26.1 1.8 %copy.11 = f32[2,8,32,128]{3,1,2,0:T(8,128)} copy(f32[2,8,32,128]{3,2,1,0:T(8,128)} %bitcast.4) | data formatting | bytes 524288

commit v5 on v4

--- a/solution.py
+++ b/solution.py
@@ -383,6 +383,16 @@
     h, m, l = me // 4, (me // 2) % 2, me % 2
     sent = []
 
+    def partner(d, back):
+        if high & (high - 1):
+            return lax.rem(h + (high - d if back else d), high)
+        a, bit = h, 1
+        while bit < high:
+            if d & bit:
+                a = a + bit - 2 * bit * ((a // bit) % 2)
+            bit *= 2
+        return a
+
     def ident(a, b, c):
         return a * 4 + b * 2 + c
 
@@ -416,26 +426,26 @@
         finish_half(w)
         pass_on(me, w, mid)
         for d in range(1, high):
-            pass_on(me, w, ident(lax.rem(h + d, high), m, l))
+            pass_on(me, w, ident(partner(d, False), m, l))
         pass_on(me, w, low)
     for w in range(2):
         b = ident(h, 1 - m, l)
         arrive(b, w)
         pass_on(b, w, low)
         for d in range(1, high):
-            a = lax.rem(h + high - d, high)
+            a = partner(d, True)
             b = ident(a, m, l)
             arrive(b, w)
             pass_on(b, w, mid)
             pass_on(b, w, low)
     for w in range(2):
         for d in range(1, high):
-            b = ident(lax.rem(h + high - d, high), 1 - m, l)
+            b = ident(partner(d, True), 1 - m, l)
             arrive(b, w)
             pass_on(b, w, low)
     for w in range(2):
         for d in range(high):
-            a = lax.rem(h + high - d, high)
+            a = partner(d, True)
             arrive(ident(a, m, 1 - l), w)
             arrive(ident(a, 1 - m, 1 - l), w)
 

time: 28 us -> 28 us (level)
  no operation moved by 1% of the time
where the time goes in v5:
time: 28 us; the launch traced here: 27.8 us
  Pallas kernels  26 us (93%)
  local copies, waits for them, and re-layouts  1.81 us (6%)
    pallas_call x1, Pallas kernels, per_device(): pl.pallas_call(functools.partial(kernel, n), out_shape=jax.ShapeDtypeStru...  26 us
    unnamed x1, local copies, waits for them, and re-layouts  1.81 us

profile of v5, /device:TPU:0, one launch (start us, length us, event | category | flops | bytes accessed | tf_op | source)
XLA Modules:
  0.0 27.8 jit_solution(126364049814381275)
XLA Ops:
  0.0 26.0 %imaging.1 = f32[16,32,128]{2,1,0:T(8,128)} custom-call(f32[2,4,2,128,512]{4,3,2,1,0:T(8,128)} %wav.1, f32[128,512]{1,0:T(8,128)} %courant.1, f32[128,512]{1,0:T(8,128)} %epsilon.1, f32[128,512]{1,0:T(8,128)} %delta.1, f32[128,512]{1,0:T(8,128)} %tilt.1, s32[256]{0:T(256)} %loc.1, s32[16]{0:T(128)} %counts.1, s32[64]{0:T(128)} %angle.1), custom_call_target="tpu_custom_call" | custom-call | tf_op jit(solution)/shard_map/imaging/pallas_call | solution.py:482
  26.0 1.8 %copy.11 = f32[2,8,32,128]{3,1,2,0:T(8,128)} copy(f32[2,8,32,128]{3,2,1,0:T(8,128)} %bitcast.4) | data formatting | bytes 524288
